TPU v7x, 128 devices: a whole 4x4x4 slice. The times are simulated.
128 devices in a mesh: seq: 16 (over x, z), head: 8 (over y, core).
Axes of the slice: x: 4, y: 4, z: 4, core: 2. Of those that a mesh axis runs over, the one named last changes fastest.
Arguments:
- tokens: bfloat16 [32768, 1024], P(('seq', 'head')), may hold values from -6 to 6
- norm_gain: float32 [1024], replicated, may hold values from 0.5 to 1.5
- w_qkv: bfloat16 [1024, 8, 384], P(None, 'head'), may hold values from -0.1875 to 0.1875
- w_mem_gates: bfloat16 [8, 3, 128], P('head'), may hold values from -0.5 to 0.5
- persist_keys: bfloat16 [16, 1024], P(None, 'head'), may hold values from -6 to 6
- persist_values: bfloat16 [16, 1024], P(None, 'head'), may hold values from -6 to 6
- alpha_bias: float32 [8], P('head'), may hold values from -8 to -2
- eta_bias: float32 [8], P('head'), may hold values from -1 to 3
- w_out: bfloat16 [1024, 1024], P('head'), may hold values from -0.1875 to 0.1875
- ffn_gain: float32 [1024], replicated, may hold values from 0.5 to 1.5
- w_gate: bfloat16 [1024, 2816], replicated, may hold values from -0.1875 to 0.1875
- w_up: bfloat16 [1024, 2816], replicated, may hold values from -0.1875 to 0.1875
- w_down: bfloat16 [2816, 1024], replicated, may hold values from -0.109375 to 0.109375
- segment_ids: int32 [32768], replicated, may hold values from 0 to 3, as said below
- block_table: int32 [512], replicated, may hold values from 0 to 511, as said below
Outputs:
- mixed: bfloat16 [32768, 1024], P(('seq', 'head'))
- kv_cache: bfloat16 [512, 64, 2048], P('seq', None, 'head')
Inputs may be any that keep to these rules, and one draw needn't show every extreme that they name: `segment_ids`: segment numbers never fall along the stream and change only at multiples of 64 tokens; all 4 numbers occur, and one prompt holds exactly 16384 tokens. `block_table`: A permutation of the cache rows. Row r belongs to owner r // 32; the 32 blocks of each index of seq (blocks i * 32 to (i + 1) * 32 - 1) put exactly 2 blocks with every owner.
All inputs are finite; a program needn't handle non-finite values.
Results may differ from a plain program's by a relative error of at most 0.02.
Values may be sent and summed in bfloat16 or wider, within the bound.
A program may use at most 128 MiB of HBM per device.

v0:
```python
import jax
import jax.numpy as jnp
from jax import lax
from jax.experimental import pallas as pl
from jax.experimental.pallas import tpu as pltpu
from jax.sharding import PartitionSpec as P

D = 1024
HD = 128
FF = 2816
PERS = 16
SPAN = 64
ROWS = 256
BPS = 32
EPS = 1e-05
TINY = 1e-06
MIB = 1 << 20
MESH = pl.DeviceIdType.MESH
F32 = jnp.float32
BF16 = jnp.bfloat16


def sigmoid(x):
    return 1.0 / (1.0 + jnp.exp(-x))


def unit(x):
    return x * lax.rsqrt(jnp.mean(x * x, axis=-1, keepdims=True) + TINY)


def mm(a, b):
    return jnp.dot(a.astype(BF16), b.astype(BF16), preferred_element_type=F32)


def compose(later, earlier):
    joined = mm(later[:, :256], earlier)
    return joined[:, :256], joined[:, 256:] + later[:, 256:]


def layer_kernel(
    keep_ref, order_ref, ab_ref, eb_ref,
    tokens_ref, ngain_ref, wq_ref, wmg_ref, pk_ref, pv_ref, wout_ref, fgain_ref,
    wg_hbm, wu_hbm, wd_hbm,
    mixed_ref, kv_hbm,
    xg, wo, wg, wu, wd, kvbuf, kvsend, rm, rs, pt, gmap, pz, srow, sin, ysend, xin,
    retsend, ret, resid, acc, ffn_in,
    local_sem, kvl_sem, xs_sem, xy_sem, xc_sem, ws_sem, wy_sem, wc_sem,
    gs_sem, gr_sem, hs_sem, hr_sem, as_sem, ar_sem, ks_sem, kr_sem,
):
    seq = lax.axis_index("seq")
    head = lax.axis_index("head")
    sx, sz = seq // 4, seq % 4
    y, c = head // 2, head % 2
    up = ((y + 1) % 4) * 2 + c
    down = ((y + 3) % 4) * 2 + c
    twin = y * 2 + (1 - c)
    znext = sx * 4 + (sz + 1) % 4
    zprev = sx * 4 + (sz + 3) % 4
    xnext = ((sx + 1) % 4) * 4 + sz

    def remote(src, dst, ssem, rsem, s, h):
        return pltpu.make_async_remote_copy(
            src_ref=src, dst_ref=dst, send_sem=ssem, recv_sem=rsem, device_id=(s, h), device_id_type=MESH
        )

    loads = [
        pltpu.make_async_copy(wg_hbm, wg, local_sem.at[0]),
        pltpu.make_async_copy(wu_hbm, wu, local_sem.at[1]),
        pltpu.make_async_copy(wd_hbm, wd, local_sem.at[2]),
    ]

    barrier = pltpu.get_barrier_semaphore()

    def greet_head(o, _):
        pl.semaphore_signal(barrier, inc=1, device_id=(seq, (head + o) % 8), device_id_type=MESH)
        return 0

    def greet_seq(o, _):
        pl.semaphore_signal(barrier, inc=1, device_id=((seq + o) % 16, head), device_id_type=MESH)
        return 0

    lax.fori_loop(1, 8, greet_head, 0)
    lax.fori_loop(1, 16, greet_seq, 0)

    tok = tokens_ref[...].astype(F32)
    scale = lax.rsqrt(jnp.mean(tok * tok, axis=-1, keepdims=True) + EPS)
    xg[head] = (tok * scale * ngain_ref[...]).astype(BF16)

    pl.semaphore_wait(barrier, 22)

    mine = xg.at[head]
    x_twin = remote(mine, mine, xs_sem.at[0], xc_sem.at[0], seq, twin)
    x_up = remote(mine, mine, xs_sem.at[1], xy_sem.at[1], seq, up)
    x_down = remote(mine, mine, xs_sem.at[2], xy_sem.at[2], seq, down)
    x_up.start()
    x_down.start()
    x_twin.start()
    for load in loads:
        load.start()

    initial = jnp.dot(
        pk_ref[...].astype(F32).T.astype(BF16), pv_ref[...], preferred_element_type=F32
    ) * (1.0 / PERS)
    row = lax.broadcasted_iota(jnp.int32, (HD, 3 * HD), 0)
    col = lax.broadcasted_iota(jnp.int32, (HD, 3 * HD), 1)
    eye_m = (row == col).astype(F32)
    eye_s = (row + HD == col).astype(F32)
    zero_wide = jnp.zeros((HD, 2 * HD), F32)
    fresh = jnp.concatenate([zero_wide, initial], axis=1)
    zero_rows = jnp.zeros((SPAN, 2 * HD), F32)

    def arrive(p, _):
        off = jnp.where(p == 1, 3, jnp.where(p == 2, 1, jnp.where(p == 3, 2, 0)))
        yp = (y + off) % 4
        slot = xg.at[2 * yp + c]
        other = xg.at[2 * yp + 1 - c]

        @pl.when(p > 0)
        def _():
            remote(slot, slot, xs_sem.at[0], xy_sem.at[p], seq, up).wait_recv()

        @pl.when(p == 1)
        def _():
            half = xg.at[2 * yp + c, pl.ds(0, ROWS // 2)]
            remote(half, half, xs_sem.at[3], xy_sem.at[3], seq, up).start()

        @pl.when(p == 2)
        def _():
            half = xg.at[2 * yp + c, pl.ds(ROWS // 2, ROWS // 2)]
            remote(half, half, xs_sem.at[4], xy_sem.at[3], seq, down).start()

        @pl.when(p > 0)
        def _():
            remote(slot, slot, xs_sem.at[4 + p], xc_sem.at[p], seq, twin).start()

        remote(other, other, xs_sem.at[0], xc_sem.at[p], seq, twin).wait_recv()

        x = xg[pl.ds(2 * yp, 2)].reshape(2 * ROWS, D)
        proj = jnp.dot(x, wq_ref[...], preferred_element_type=F32)
        q = unit(proj[:, :HD]) * HD ** (-0.5)
        k = unit(proj[:, HD : 2 * HD]) * HD ** (-0.5)
        v = proj[:, 2 * HD :]
        wmg = wmg_ref[...].astype(F32)
        theta = sigmoid(jnp.sum(v * wmg[0:1], axis=-1, keepdims=True)) * (1.0 / SPAN)
        mean_v = jnp.mean(v.reshape(8, SPAN, HD), axis=1)
        alpha = sigmoid(jnp.sum(mean_v * wmg[1:2], axis=-1, keepdims=True) + ab_ref[0])
        eta = sigmoid(jnp.sum(mean_v * wmg[2:3], axis=-1, keepdims=True) + eb_ref[0])
        qb, kb = q.astype(BF16), k.astype(BF16)
        kvbuf[pl.ds(yp * 8, 8), :, :HD] = kb.reshape(8, SPAN, HD)
        kvbuf[pl.ds(yp * 8, 8), :, HD:] = v.astype(BF16).reshape(8, SPAN, HD)

        state = [(eye_m, eye_s), (eye_m, eye_s)]
        reads = [[], []]
        for step in range(4):
            for half in range(2):
                b = half * 4 + step
                rows = slice(b * SPAN, (b + 1) * SPAN)
                memory, moment = state[half]
                keep = keep_ref[yp * 8 + b]
                held = keep * memory + (1.0 - keep) * fresh
                both = mm(jnp.concatenate([qb[rows], kb[rows]], axis=0), held)
                reads[half].append(both[:SPAN])
                wide_v = jnp.concatenate([zero_rows, v[rows]], axis=1)
                push = theta[rows] * (wide_v - both[SPAN:])
                moment = eta[b : b + 1] * (keep * moment) + mm(k[rows].T, push)
                memory = (1.0 - alpha[b : b + 1]) * held + moment
                state[half] = (memory, moment)
        even = jnp.concatenate(state[0], axis=0)
        odd = jnp.concatenate(state[1], axis=0)
        tmap, tshift = compose(odd, even)
        pt[yp, :, :256] = tmap
        pt[yp, :, 256:] = tshift
        read_even = jnp.concatenate(reads[0], axis=0)
        read_odd = jnp.concatenate(reads[1], axis=0)
        omap, oshift = compose(read_odd, even)
        rm[2 * yp] = read_even[:, :256].astype(BF16)
        rs[2 * yp] = read_even[:, 256:]
        rm[2 * yp + 1] = omap.astype(BF16)
        rs[2 * yp + 1] = oshift
        return 0

    lax.fori_loop(0, 4, arrive, 0)

    def join(later, earlier):
        return jnp.concatenate(compose(later, earlier), axis=1)

    first = join(pt[1], pt[0])
    total = join(join(pt[3], pt[2]), first)
    gmap[sz] = total.astype(BF16)
    gmine = gmap.at[sz]
    remote(gmine, gmine, gs_sem.at[0], gr_sem.at[1], znext, head).start()
    remote(gmine, gmine, gs_sem.at[1], gr_sem.at[2], zprev, head).start()

    wo[head] = wout_ref[...]
    wmine = wo.at[head]
    remote(wmine, wmine, ws_sem.at[1], wy_sem.at[1], seq, up).start()
    remote(wmine, wmine, ws_sem.at[2], wy_sem.at[2], seq, down).start()
    remote(wmine, wmine, ws_sem.at[0], wc_sem.at[0], seq, twin).start()

    def fold(p, emap):
        read = rm[pl.ds(2 * p, 2)].reshape(2 * ROWS, 2 * HD)
        out = jnp.dot(read, emap.astype(BF16), preferred_element_type=F32)
        rm[pl.ds(2 * p, 2)] = out[:, :256].astype(BF16).reshape(2, ROWS, 2 * HD)
        rs[pl.ds(2 * p, 2)] = rs[pl.ds(2 * p, 2)] + out[:, 256:].reshape(2, ROWS, HD)

    fold(1, pt[0])
    fold(2, first)
    fold(3, join(pt[2], first))

    def place(p, _):
        kvsend[p] = kvbuf[order_ref[p]]
        return 0

    lax.fori_loop(0, BPS, place, 0)

    def gslot(step):
        return gmap.at[(sz + step) % 4]

    remote(gslot(3), gslot(3), gs_sem.at[0], gr_sem.at[1], znext, head).wait_recv()
    half = gmap.at[(sz + 3) % 4, pl.ds(0, 128)]
    remote(half, half, gs_sem.at[2], gr_sem.at[3], znext, head).start()
    remote(gslot(1), gslot(1), gs_sem.at[0], gr_sem.at[2], znext, head).wait_recv()
    half = gmap.at[(sz + 1) % 4, pl.ds(128, 128)]
    remote(half, half, gs_sem.at[3], gr_sem.at[3], zprev, head).start()
    remote(gslot(2), gslot(2), gs_sem.at[0], gr_sem.at[3], znext, head).wait_recv()

    def bjoin(later, earlier):
        tmap, tshift = compose(later.astype(F32), earlier)
        return jnp.concatenate([tmap, tshift], axis=1)

    low = bjoin(gmap[1], gmap[0])
    total = join(bjoin(gmap[3], gmap[2]), low)
    srow[...] = total[:, 256:].astype(BF16)
    remote(srow, sin, hs_sem.at[0], hr_sem.at[0], xnext, head).start()

    @pl.when(sz == 1)
    def _():
        pz[...] = gmap[0]

    @pl.when(sz == 2)
    def _():
        pz[...] = low.astype(BF16)

    @pl.when(sz == 3)
    def _():
        pz[...] = bjoin(gmap[2], low).astype(BF16)

    wprev, wnext = wo.at[((y + 3) % 4) * 2 + c], wo.at[((y + 1) % 4) * 2 + c]
    remote(wprev, wprev, ws_sem.at[1], wy_sem.at[1], seq, up).wait_recv()
    half = wo.at[((y + 3) % 4) * 2 + c, pl.ds(0, 64)]
    remote(half, half, ws_sem.at[3], wy_sem.at[3], seq, up).start()
    remote(wprev, wprev, ws_sem.at[5], wc_sem.at[1], seq, twin).start()
    remote(wnext, wnext, ws_sem.at[1], wy_sem.at[2], seq, up).wait_recv()
    half = wo.at[((y + 1) % 4) * 2 + c, pl.ds(64, 64)]
    remote(half, half, ws_sem.at[4], wy_sem.at[3], seq, down).start()
    remote(wnext, wnext, ws_sem.at[6], wc_sem.at[2], seq, twin).start()

    remote(srow, sin, hs_sem.at[0], hr_sem.at[0], xnext, head).wait_recv()
    ysend[...] = (mm(total[:, :256], sin[...]) + total[:, 256:]).astype(BF16)
    remote(ysend, xin, hs_sem.at[1], hr_sem.at[1], xnext, head).start()

    @pl.when(sz > 0)
    def _():
        def fold_all(p, _):
            fold(p, pz[...])
            return 0

        lax.fori_loop(0, 4, fold_all, 0)

    def kv_copy(o):
        to = (seq + o) % 16
        return remote(
            kvsend.at[pl.ds(2 * to, 2)], kv_hbm.at[pl.ds(2 * seq, 2)], ks_sem.at[o], kr_sem.at[o], to, head
        )

    def kv_arrival(o):
        source = (seq + 16 - o) % 16
        return remote(
            kvsend.at[pl.ds(2 * source, 2)], kv_hbm.at[pl.ds(2 * source, 2)], ks_sem.at[o], kr_sem.at[o], source, head
        )

    def kv_start(o, _):
        kv_copy(o).start()
        return 0

    lax.fori_loop(1, 16, kv_start, 0)
    kv_own = pltpu.make_async_copy(kvsend.at[pl.ds(2 * seq, 2)], kv_hbm.at[pl.ds(2 * seq, 2)], kvl_sem)
    kv_own.start()

    wfar = wo.at[((y + 2) % 4) * 2 + c]
    remote(wfar, wfar, ws_sem.at[1], wy_sem.at[3], seq, up).wait_recv()
    remote(wfar, wfar, ws_sem.at[7], wc_sem.at[3], seq, twin).start()

    remote(ysend, xin, hs_sem.at[1], hr_sem.at[1], xnext, head).wait_recv()
    enter = xin[...]

    def answer(j):
        recalled = jnp.dot(rm[j], enter, preferred_element_type=F32) + rs[j]
        return unit(recalled).astype(BF16)

    def ret_copy(oy, oc):
        o = oy * 2 + oc
        to = ((y + oy) % 4) * 2 + (c + oc) % 2
        return remote(retsend.at[o], ret.at[head], as_sem.at[o], ar_sem.at[o], seq, to)

    def ret_arrival(oy, oc):
        o = oy * 2 + oc
        source = ((y + 4 - oy) % 4) * 2 + (c + oc) % 2
        return remote(retsend.at[o], ret.at[source], as_sem.at[o], ar_sem.at[o], seq, source)

    turns = [(2, 0), (2, 1), (1, 0), (1, 1), (3, 0), (3, 1), (0, 1)]
    for oy, oc in turns:
        retsend[oy * 2 + oc] = answer(((y + oy) % 4) * 2 + (c + oc) % 2)
        ret_copy(oy, oc).start()
    ret[head] = answer(head)

    for p, off in ((0, 0), (1, 3), (2, 1), (3, 2)):
        other = wo.at[((y + off) % 4) * 2 + 1 - c]
        remote(other, other, ws_sem.at[0], wc_sem.at[p], seq, twin).wait_recv()
    for load in loads:
        load.wait()
    for oy, oc in turns:
        ret_arrival(oy, oc).wait_recv()

    total = tokens_ref[...].astype(F32)
    for i in range(4):
        left = jnp.concatenate([ret[2 * i], ret[2 * i + 1]], axis=1)
        total = total + jnp.dot(left, wo[2 * i : 2 * i + 2].reshape(2 * HD, D), preferred_element_type=F32)
    acc[...] = total
    scale = lax.rsqrt(jnp.mean(total * total, axis=-1, keepdims=True) + EPS)
    ffn_in[...] = (total * scale * fgain_ref[...]).astype(BF16)

    def ffn(t, _):
        cols = pl.ds(pl.multiple_of(t * 256, 256), 256)
        gate = jnp.dot(ffn_in[...], wg[:, cols], preferred_element_type=F32)
        upper = jnp.dot(ffn_in[...], wu[:, cols], preferred_element_type=F32)
        hidden = (gate / (1.0 + jnp.exp(-gate)) * upper).astype(BF16)
        acc[...] += jnp.dot(hidden, wd[cols, :], preferred_element_type=F32)
        return 0

    lax.fori_loop(0, FF // 256, ffn, 0)
    mixed_ref[...] = acc[...].astype(BF16)

    def kv_end(o, _):
        kv_arrival(o).wait_recv()
        kv_copy(o).wait_send()
        return 0

    lax.fori_loop(1, 16, kv_end, 0)
    kv_own.wait()
    whole = xg.at[head]
    for i in (0, 1, 2, 5, 6, 7):
        remote(whole, whole, xs_sem.at[i], xy_sem.at[1], seq, up).wait_send()
    half = xg.at[head, pl.ds(0, ROWS // 2)]
    for i in (3, 4):
        remote(half, half, xs_sem.at[i], xy_sem.at[1], seq, up).wait_send()
    for i in (0, 1, 2, 5, 6, 7):
        remote(wmine, wmine, ws_sem.at[i], wy_sem.at[1], seq, up).wait_send()
    half = wo.at[head, pl.ds(0, 64)]
    for i in (3, 4):
        remote(half, half, ws_sem.at[i], wy_sem.at[1], seq, up).wait_send()
    for i in (0, 1):
        remote(gmine, gmine, gs_sem.at[i], gr_sem.at[1], znext, head).wait_send()
    half = gmap.at[sz, pl.ds(0, 128)]
    for i in (2, 3):
        remote(half, half, gs_sem.at[i], gr_sem.at[1], znext, head).wait_send()
    remote(srow, sin, hs_sem.at[0], hr_sem.at[0], xnext, head).wait_send()
    remote(ysend, xin, hs_sem.at[1], hr_sem.at[1], xnext, head).wait_send()
    for oy, oc in turns:
        ret_copy(oy, oc).wait_send()


def per_device(
    tokens, norm_gain, w_qkv, w_mem_gates, persist_keys, persist_values, alpha_bias, eta_bias,
    w_out, ffn_gain, w_gate, w_up, w_down, segment_ids, block_table,
):
    seq = lax.axis_index("seq")
    ids = segment_ids.reshape(-1, SPAN)[:, 0]
    keep_all = jnp.concatenate([jnp.zeros((1,), F32), (ids[1:] == ids[:-1]).astype(F32)])
    keep = lax.dynamic_slice_in_dim(keep_all, seq * BPS, BPS)
    slots = jnp.arange(BPS, dtype=jnp.int32)
    mine = lax.dynamic_slice_in_dim(block_table, seq * BPS, BPS)
    place = (mine // BPS) * BPS + slots
    position = jnp.sum((place[None, :] < place[:, None]).astype(jnp.int32), axis=1)
    order = jnp.sum(jnp.where(position[None, :] == slots[:, None], slots[None, :], 0), axis=1)

    vmem = pl.BlockSpec(memory_space=pltpu.VMEM)
    smem = pl.BlockSpec(memory_space=pltpu.SMEM)
    anywhere = pl.BlockSpec(memory_space=pl.ANY)
    dma = pltpu.SemaphoreType.DMA
    mixed, arrived = pl.pallas_call(
        layer_kernel,
        out_shape=(
            jax.ShapeDtypeStruct((ROWS, D), BF16),
            jax.ShapeDtypeStruct((BPS, SPAN, 2 * HD), BF16),
        ),
        in_specs=[smem] * 4 + [vmem] * 8 + [anywhere] * 3,
        out_specs=(vmem, anywhere),
        scratch_shapes=[
            pltpu.VMEM((8, ROWS, D), BF16),
            pltpu.VMEM((8, HD, D), BF16),
            pltpu.VMEM((D, FF), BF16),
            pltpu.VMEM((D, FF), BF16),
            pltpu.VMEM((FF, D), BF16),
            pltpu.VMEM((BPS, SPAN, 2 * HD), BF16),
            pltpu.VMEM((BPS, SPAN, 2 * HD), BF16),
            pltpu.VMEM((8, ROWS, 2 * HD), BF16),
            pltpu.VMEM((8, ROWS, HD), F32),
            pltpu.VMEM((4, 2 * HD, 3 * HD), F32),
            pltpu.VMEM((4, 2 * HD, 3 * HD), BF16),
            pltpu.VMEM((2 * HD, 3 * HD), BF16),
            pltpu.VMEM((2 * HD, HD), BF16),
            pltpu.VMEM((2 * HD, HD), BF16),
            pltpu.VMEM((2 * HD, HD), BF16),
            pltpu.VMEM((2 * HD, HD), BF16),
            pltpu.VMEM((8, ROWS, HD), BF16),
            pltpu.VMEM((8, ROWS, HD), BF16),
            pltpu.VMEM((8, HD), F32),
            pltpu.VMEM((ROWS, D), F32),
            pltpu.VMEM((ROWS, D), BF16),
            dma((3,)), dma,
            dma((8,)), dma((4,)), dma((4,)),
            dma((8,)), dma((4,)), dma((4,)),
            dma((4,)), dma((4,)),
            dma((2,)), dma((2,)),
            dma((8,)), dma((8,)),
            dma((16,)), dma((16,)),
        ],
        compiler_params=pltpu.CompilerParams(
            collective_id=0, has_side_effects=True, vmem_limit_bytes=56 * MIB
        ),
    )(
        keep, order, alpha_bias, eta_bias,
        tokens, norm_gain.reshape(1, D), w_qkv.reshape(D, 3 * HD), w_mem_gates.reshape(3, HD),
        persist_keys, persist_values, w_out, ffn_gain.reshape(1, D),
        w_gate, w_up, w_down,
    )

    wanted = seq * BPS + slots
    blocks = jnp.arange(block_table.shape[0], dtype=jnp.int32)
    block_of = jnp.sum(jnp.where(block_table[None, :] == wanted[:, None], blocks[None, :], 0), axis=1)
    spot = jnp.sum((block_of[None, :] < block_of[:, None]).astype(jnp.int32), axis=1)
    return mixed, arrived[spot]


def solution(mesh):
    return jax.shard_map(
        per_device,
        mesh=mesh,
        in_specs=(
            P(("seq", "head"), None),
            P(),
            P(None, "head", None),
            P("head", None, None),
            P(None, "head"),
            P(None, "head"),
            P("head"),
            P("head"),
            P("head", None),
            P(),
            P(),
            P(),
            P(),
            P(),
            P(),
        ),
        out_specs=(P(("seq", "head"), None), P("seq", None, "head")),
        check_vma=False,
    )
```

profile of v0, /device:TPU:1, one launch (start us, length us, event | category | flops | bytes accessed | tf_op | source)
XLA Modules:
  0.0 84.2 jit_solution(964919468951003074)
XLA Ops:
  1.9 0.9 %select_reduce_fusion = s32[32]{0:T(128)S(1)} fusion(s32[512]{0:T(512)} %param.29, s32[32]{0:T(128)S(1)} %iota_add_fusion), kind=kLoop, calls=%fused_computation.3 | loop fusion | flops 49120 | bytes 2304 | tf_op jit(solution)/shard_map/reduce_sum | solution.py:441
  2.8 0.2 convert_reduce_fusion
  3.0 0.8 iota_add_fusion.1
  3.8 0.2 convert_reduce_fusion.1
  3.9 0.6 select_reduce_fusion.1.order_ref
  4.6 1.0 %reshape.47 = s32[512,64]{1,0:T(8,128)S(1)} reshape(s32[32768]{0:T(1024)} %param.28) | data formatting | bytes 262144 | tf_op jit(solution)/shard_map/reshape | solution.py:378
  5.6 0.1 fusion
  5.8 0.1 add_convert_fusion
  5.8 0.6 dynamic_slice.6.keep_ref
  6.4 73.1 %shard_map.158 = (bf16[256,1024]{1,0:T(8,128)(2,1)}, bf16[32,64,256]{2,1,0:T(8,128)(2,1)}) custom-call(f32[32]{0:T(128)} %dynamic_slice.6.keep_ref, s32[32]{0:T(128)} %select_reduce_fusion.1.order_ref, f32[1]{0:T(128)S(6)} %copy.18.ab_ref, f32[1]{0:T(128)S(6)} %copy.19.eb_ref, bf16[256,1024]{1,0:T(8,128)(2,1)} %tokens_ref.1, f32[1,1024]{1,0:T(1,128)} %bitcast.9, ...), custom_call_target="tpu_custom_call" | custom-call | tf_op jit(solution)/shard_map/pallas_call | solution.py:391
  79.5 2.8 %gather_fusion = bf16[32,64,256]{2,1,0:T(8,128)(2,1)} fusion(bf16[32,64,256]{2,1,0:T(8,128)(2,1)} %get-tuple-element.5, s32[1024]{0:T(1024)S(1)} %pad_clamp_fusion), kind=kCustom, calls=%fused_computation | custom fusion | bytes 2097280 | tf_op jit(solution)/shard_map/gather | solution.py:443
  82.3 1.9 %copy.20 = bf16[256,1024]{1,0:T(8,128)(2,1)} copy(bf16[256,1024]{1,0:T(8,128)(2,1)} %get-tuple-element.8) | data formatting | bytes 1048576
  (3 shorter events, 0.0 us)
where the time goes:
time: 84.5 us; the launch traced here: 84.2 us
  Pallas kernels  73.1 us (87%)
  local copies, waits for them, and re-layouts  6.27 us (7%)
  other arithmetic  2.87 us (3%)
  between operations  1.97 us (2%)
    pallas_call x1, Pallas kernels, per_device(): pl.pallas_call(layer_kernel, out_shape=(jax.ShapeDtypeStruct((ROWS, D), B...  73.1 us
    gather x1, local copies, waits for them, and re-layouts, per_device(): return (mixed, arrived[spot])  2.81 us
    unnamed x1, local copies, waits for them, and re-layouts  1.87 us

commit v1 on v0

--- a/solution.py
+++ b/solution.py
@@ -11,6 +11,8 @@
 PERS = 16
 SPAN = 64
 ROWS = 256
+PIECE = 64
+TOKENS = 32768
 BPS = 32
 EPS = 1e-05
 TINY = 1e-06
@@ -38,13 +40,13 @@
 
 
 def layer_kernel(
-    keep_ref, order_ref, ab_ref, eb_ref,
-    tokens_ref, ngain_ref, wq_ref, wmg_ref, pk_ref, pv_ref, wout_ref, fgain_ref,
+    ab_ref, eb_ref, table_ref, ids_hbm,
+    wide_table_ref, tokens_ref, ngain_ref, wq_ref, wmg_ref, pk_ref, pv_ref, wout_ref, fgain_ref,
     wg_hbm, wu_hbm, wd_hbm,
-    mixed_ref, kv_hbm,
-    xg, wo, wg, wu, wd, kvbuf, kvsend, rm, rs, pt, gmap, pz, srow, sin, ysend, xin,
-    retsend, ret, resid, acc, ffn_in,
-    local_sem, kvl_sem, xs_sem, xy_sem, xc_sem, ws_sem, wy_sem, wc_sem,
+    mixed_ref, kv_hbm, rowof_ref,
+    ids, before, order, xg, wo, wg, wu, wd, kvbuf, kvsend, rm, rs, pt, gmap, pz, srow, sin, ysend, xin,
+    retsend, ret, resid, ffn_in, hid,
+    local_sem, kvl_sem, own_sem, fwd_sem, tws_sem, yr_sem, twr_sem, ws_sem, wy_sem, wc_sem,
     gs_sem, gr_sem, hs_sem, hr_sem, as_sem, ar_sem, ks_sem, kr_sem,
 ):
     seq = lax.axis_index("seq")
@@ -68,6 +70,14 @@
         pltpu.make_async_copy(wu_hbm, wu, local_sem.at[1]),
         pltpu.make_async_copy(wd_hbm, wd, local_sem.at[2]),
     ]
+    mine_ids = pl.multiple_of(seq * (BPS * SPAN), 1024)
+    prior_ids = pl.multiple_of((seq * (BPS * SPAN) + TOKENS - 1024) % TOKENS, 1024)
+    id_loads = [
+        pltpu.make_async_copy(ids_hbm.at[pl.ds(mine_ids, BPS * SPAN)], ids, local_sem.at[3]),
+        pltpu.make_async_copy(ids_hbm.at[pl.ds(prior_ids, 1024)], before, local_sem.at[4]),
+    ]
+    for load in id_loads:
+        load.start()
 
     barrier = pltpu.get_barrier_semaphore()
 
@@ -88,13 +98,24 @@
 
     pl.semaphore_wait(barrier, 22)
 
-    mine = xg.at[head]
-    x_twin = remote(mine, mine, xs_sem.at[0], xc_sem.at[0], seq, twin)
-    x_up = remote(mine, mine, xs_sem.at[1], xy_sem.at[1], seq, up)
-    x_down = remote(mine, mine, xs_sem.at[2], xy_sem.at[2], seq, down)
-    x_up.start()
-    x_down.start()
-    x_twin.start()
+    def piece(slot, i):
+        return xg.at[slot, pl.ds(i * PIECE, PIECE)]
+
+    def y_copy(slot, i, sem, kind, to):
+        part = piece(slot, i)
+        return remote(part, part, sem, yr_sem.at[kind, i], seq, to)
+
+    def twin_copy(slot, i, kind):
+        part = piece(slot, i)
+        return remote(part, part, tws_sem.at[kind, i], twr_sem.at[kind, i], seq, twin)
+
+    slots = [2 * ((y + off) % 4) + c for off in (0, 3, 1, 2)]
+    others = [2 * ((y + off) % 4) + 1 - c for off in (0, 3, 1, 2)]
+    for i in range(4):
+        y_copy(head, i, own_sem.at[0, i], 1, up).start()
+        y_copy(head, 3 - i, own_sem.at[1, 3 - i], 2, down).start()
+    for i in range(4):
+        twin_copy(head, i, 0).start()
     for load in loads:
         load.start()
 
@@ -109,77 +130,104 @@
     fresh = jnp.concatenate([zero_wide, initial], axis=1)
     zero_rows = jnp.zeros((SPAN, 2 * HD), F32)
 
-    def arrive(p, _):
-        off = jnp.where(p == 1, 3, jnp.where(p == 2, 1, jnp.where(p == 3, 2, 0)))
-        yp = (y + off) % 4
-        slot = xg.at[2 * yp + c]
-        other = xg.at[2 * yp + 1 - c]
-
-        @pl.when(p > 0)
-        def _():
-            remote(slot, slot, xs_sem.at[0], xy_sem.at[p], seq, up).wait_recv()
-
-        @pl.when(p == 1)
-        def _():
-            half = xg.at[2 * yp + c, pl.ds(0, ROWS // 2)]
-            remote(half, half, xs_sem.at[3], xy_sem.at[3], seq, up).start()
-
-        @pl.when(p == 2)
-        def _():
-            half = xg.at[2 * yp + c, pl.ds(ROWS // 2, ROWS // 2)]
-            remote(half, half, xs_sem.at[4], xy_sem.at[3], seq, down).start()
-
-        @pl.when(p > 0)
-        def _():
-            remote(slot, slot, xs_sem.at[4 + p], xc_sem.at[p], seq, twin).start()
-
-        remote(other, other, xs_sem.at[0], xc_sem.at[p], seq, twin).wait_recv()
-
-        x = xg[pl.ds(2 * yp, 2)].reshape(2 * ROWS, D)
-        proj = jnp.dot(x, wq_ref[...], preferred_element_type=F32)
-        q = unit(proj[:, :HD]) * HD ** (-0.5)
-        k = unit(proj[:, HD : 2 * HD]) * HD ** (-0.5)
-        v = proj[:, 2 * HD :]
-        wmg = wmg_ref[...].astype(F32)
-        theta = sigmoid(jnp.sum(v * wmg[0:1], axis=-1, keepdims=True)) * (1.0 / SPAN)
-        mean_v = jnp.mean(v.reshape(8, SPAN, HD), axis=1)
-        alpha = sigmoid(jnp.sum(mean_v * wmg[1:2], axis=-1, keepdims=True) + ab_ref[0])
-        eta = sigmoid(jnp.sum(mean_v * wmg[2:3], axis=-1, keepdims=True) + eb_ref[0])
-        qb, kb = q.astype(BF16), k.astype(BF16)
-        kvbuf[pl.ds(yp * 8, 8), :, :HD] = kb.reshape(8, SPAN, HD)
-        kvbuf[pl.ds(yp * 8, 8), :, HD:] = v.astype(BF16).reshape(8, SPAN, HD)
-
-        state = [(eye_m, eye_s), (eye_m, eye_s)]
-        reads = [[], []]
+    wide = wide_table_ref[...]
+    place_no = lax.broadcasted_iota(jnp.int32, (4, 128), 0) * 128 + lax.broadcasted_iota(jnp.int32, (4, 128), 1)
+    owner_no = lax.shift_right_logical(wide, 5)
+    key_no = owner_no * BPS + (place_no & (BPS - 1))
+    position = jnp.zeros((4, 128), jnp.int32)
+    for i in range(BPS):
+        one = lax.shift_right_logical(table_ref[seq * BPS + i], 5) * BPS + i
+        position = position + (one < key_no).astype(jnp.int32)
+    position = jnp.where(lax.shift_right_logical(place_no, 5) == seq, position, -1)
+    owned = (owner_no == seq).astype(F32)
+    earlier = lax.broadcasted_iota(jnp.int32, (128, 128), 0) < lax.broadcasted_iota(jnp.int32, (128, 128), 1)
+    rank = mm(jnp.concatenate([owned, owned], axis=0), earlier.astype(F32))[:4]
+    rank = rank + 8.0 * lax.broadcasted_iota(jnp.int32, (4, 128), 0).astype(F32)
+    rank = jnp.where(owned > 0.0, rank, -1.0)
+    for i in range(BPS):
+        order[i] = jnp.sum(jnp.where(position == i, place_no & (BPS - 1), 0))
+        rowof_ref[i] = jnp.sum(jnp.where(rank == float(i), wide & (BPS - 1), 0))
+    for load in id_loads:
+        load.wait()
+
+    def keep_of(yp, b):
+        block = yp * 8 + b
+        here = ids[block * SPAN]
+        there = ids[jnp.maximum(block * SPAN - 1, 0)]
+        there = jnp.where(block == 0, before[1023], there)
+        there = jnp.where(block + seq == 0, -1, there)
+        return jnp.where(here == there, 1.0, 0.0)
+
+    def process(chips):
+        work = []
+        for yp in chips:
+            x = xg[pl.ds(2 * yp, 2)].reshape(2 * ROWS, D)
+            proj = jnp.dot(x, wq_ref[...], preferred_element_type=F32)
+            q = unit(proj[:, :HD]) * HD ** (-0.5)
+            k = unit(proj[:, HD : 2 * HD]) * HD ** (-0.5)
+            v = proj[:, 2 * HD :]
+            wmg = wmg_ref[...].astype(F32)
+            theta = sigmoid(jnp.sum(v * wmg[0:1], axis=-1, keepdims=True)) * (1.0 / SPAN)
+            mean_v = jnp.mean(v.reshape(8, SPAN, HD), axis=1)
+            alpha = sigmoid(jnp.sum(mean_v * wmg[1:2], axis=-1, keepdims=True) + ab_ref[0])
+            eta = sigmoid(jnp.sum(mean_v * wmg[2:3], axis=-1, keepdims=True) + eb_ref[0])
+            qb, kb = q.astype(BF16), k.astype(BF16)
+            kvbuf[pl.ds(yp * 8, 8), :, :HD] = kb.reshape(8, SPAN, HD)
+            kvbuf[pl.ds(yp * 8, 8), :, HD:] = v.astype(BF16).reshape(8, SPAN, HD)
+            for half in range(2):
+                work.append([yp, half * 4, qb, k, kb, v, theta, alpha, eta, eye_m, eye_s, []])
         for step in range(4):
-            for half in range(2):
-                b = half * 4 + step
+            for item in work:
+                yp, first_block, qb, k, kb, v, theta, alpha, eta, memory, moment, reads = item
+                b = first_block + step
                 rows = slice(b * SPAN, (b + 1) * SPAN)
-                memory, moment = state[half]
-                keep = keep_ref[yp * 8 + b]
+                keep = keep_of(yp, b)
                 held = keep * memory + (1.0 - keep) * fresh
                 both = mm(jnp.concatenate([qb[rows], kb[rows]], axis=0), held)
-                reads[half].append(both[:SPAN])
+                reads.append(both[:SPAN])
                 wide_v = jnp.concatenate([zero_rows, v[rows]], axis=1)
                 push = theta[rows] * (wide_v - both[SPAN:])
                 moment = eta[b : b + 1] * (keep * moment) + mm(k[rows].T, push)
                 memory = (1.0 - alpha[b : b + 1]) * held + moment
-                state[half] = (memory, moment)
-        even = jnp.concatenate(state[0], axis=0)
-        odd = jnp.concatenate(state[1], axis=0)
-        tmap, tshift = compose(odd, even)
-        pt[yp, :, :256] = tmap
-        pt[yp, :, 256:] = tshift
-        read_even = jnp.concatenate(reads[0], axis=0)
-        read_odd = jnp.concatenate(reads[1], axis=0)
-        omap, oshift = compose(read_odd, even)
-        rm[2 * yp] = read_even[:, :256].astype(BF16)
-        rs[2 * yp] = read_even[:, 256:]
-        rm[2 * yp + 1] = omap.astype(BF16)
-        rs[2 * yp + 1] = oshift
-        return 0
-
-    lax.fori_loop(0, 4, arrive, 0)
+                item[9], item[10] = memory, moment
+        for i in range(0, len(work), 2):
+            yp = work[i][0]
+            even = jnp.concatenate([work[i][9], work[i][10]], axis=0)
+            odd = jnp.concatenate([work[i + 1][9], work[i + 1][10]], axis=0)
+            tmap, tshift = compose(odd, even)
+            pt[yp, :, :256] = tmap
+            pt[yp, :, 256:] = tshift
+            read_even = jnp.concatenate(work[i][11], axis=0)
+            read_odd = jnp.concatenate(work[i + 1][11], axis=0)
+            omap, oshift = compose(read_odd, even)
+            rm[2 * yp] = read_even[:, :256].astype(BF16)
+            rs[2 * yp] = read_even[:, 256:]
+            rm[2 * yp + 1] = omap.astype(BF16)
+            rs[2 * yp + 1] = oshift
+
+    def twin_in(kind):
+        for i in range(4):
+            twin_copy(others[kind], i, kind).wait_recv()
+
+    twin_in(0)
+    process([y])
+    for i in range(4):
+        y_copy(slots[1], i, own_sem.at[0, 0], 1, up).wait_recv()
+        if i < 2:
+            y_copy(slots[1], i, fwd_sem.at[i], 3, up).start()
+        twin_copy(slots[1], i, 1).start()
+        y_copy(slots[2], 3 - i, own_sem.at[0, 0], 2, up).wait_recv()
+        if i < 2:
+            y_copy(slots[2], 3 - i, fwd_sem.at[3 - i], 3, down).start()
+        twin_copy(slots[2], 3 - i, 2).start()
+    twin_in(1)
+    twin_in(2)
+    process([(y + 3) % 4, (y + 1) % 4])
+    for i in (0, 3, 1, 2):
+        y_copy(slots[3], i, own_sem.at[0, 0], 3, up).wait_recv()
+        twin_copy(slots[3], i, 3).start()
+    twin_in(3)
+    process([(y + 2) % 4])
 
     def join(later, earlier):
         return jnp.concatenate(compose(later, earlier), axis=1)
@@ -187,9 +235,13 @@
     first = join(pt[1], pt[0])
     total = join(join(pt[3], pt[2]), first)
     gmap[sz] = total.astype(BF16)
-    gmine = gmap.at[sz]
-    remote(gmine, gmine, gs_sem.at[0], gr_sem.at[1], znext, head).start()
-    remote(gmine, gmine, gs_sem.at[1], gr_sem.at[2], zprev, head).start()
+    def g_copy(step, i, sem, kind, to):
+        part = gmap.at[(sz + step) % 4, pl.ds(i * HD, HD)]
+        return remote(part, part, sem, gr_sem.at[kind, i], to, head)
+
+    for i in range(2):
+        g_copy(0, i, gs_sem.at[0, i], 1, znext).start()
+        g_copy(0, 1 - i, gs_sem.at[1, 1 - i], 2, zprev).start()
 
     wo[head] = wout_ref[...]
     wmine = wo.at[head]
@@ -208,21 +260,19 @@
     fold(3, join(pt[2], first))
 
     def place(p, _):
-        kvsend[p] = kvbuf[order_ref[p]]
+        kvsend[p] = kvbuf[order[p]]
         return 0
 
     lax.fori_loop(0, BPS, place, 0)
 
-    def gslot(step):
-        return gmap.at[(sz + step) % 4]
-
-    remote(gslot(3), gslot(3), gs_sem.at[0], gr_sem.at[1], znext, head).wait_recv()
-    half = gmap.at[(sz + 3) % 4, pl.ds(0, 128)]
-    remote(half, half, gs_sem.at[2], gr_sem.at[3], znext, head).start()
-    remote(gslot(1), gslot(1), gs_sem.at[0], gr_sem.at[2], znext, head).wait_recv()
-    half = gmap.at[(sz + 1) % 4, pl.ds(128, 128)]
-    remote(half, half, gs_sem.at[3], gr_sem.at[3], zprev, head).start()
-    remote(gslot(2), gslot(2), gs_sem.at[0], gr_sem.at[3], znext, head).wait_recv()
+    g_copy(3, 0, gs_sem.at[0, 0], 1, znext).wait_recv()
+    g_copy(3, 0, gs_sem.at[2, 0], 3, znext).start()
+    g_copy(1, 1, gs_sem.at[0, 0], 2, znext).wait_recv()
+    g_copy(1, 1, gs_sem.at[2, 1], 3, zprev).start()
+    g_copy(3, 1, gs_sem.at[0, 0], 1, znext).wait_recv()
+    g_copy(1, 0, gs_sem.at[0, 0], 2, znext).wait_recv()
+    g_copy(2, 0, gs_sem.at[0, 0], 3, znext).wait_recv()
+    g_copy(2, 1, gs_sem.at[0, 0], 3, znext).wait_recv()
 
     def bjoin(later, earlier):
         tmap, tshift = compose(later.astype(F32), earlier)
@@ -326,20 +376,22 @@
     for i in range(4):
         left = jnp.concatenate([ret[2 * i], ret[2 * i + 1]], axis=1)
         total = total + jnp.dot(left, wo[2 * i : 2 * i + 2].reshape(2 * HD, D), preferred_element_type=F32)
-    acc[...] = total
+    resid[...] = total
     scale = lax.rsqrt(jnp.mean(total * total, axis=-1, keepdims=True) + EPS)
     ffn_in[...] = (total * scale * fgain_ref[...]).astype(BF16)
 
-    def ffn(t, _):
+    def widen(t, _):
         cols = pl.ds(pl.multiple_of(t * 256, 256), 256)
         gate = jnp.dot(ffn_in[...], wg[:, cols], preferred_element_type=F32)
         upper = jnp.dot(ffn_in[...], wu[:, cols], preferred_element_type=F32)
-        hidden = (gate / (1.0 + jnp.exp(-gate)) * upper).astype(BF16)
-        acc[...] += jnp.dot(hidden, wd[cols, :], preferred_element_type=F32)
+        hid[:, cols] = (gate / (1.0 + jnp.exp(-gate)) * upper).astype(BF16)
         return 0
 
-    lax.fori_loop(0, FF // 256, ffn, 0)
-    mixed_ref[...] = acc[...].astype(BF16)
+    lax.fori_loop(0, FF // 256, widen, 0)
+    for t in range(4):
+        cols = slice(t * 256, (t + 1) * 256)
+        down_part = jnp.dot(hid[...], wd[:, cols], preferred_element_type=F32)
+        mixed_ref[:, cols] = (resid[:, cols] + down_part).astype(BF16)
 
     def kv_end(o, _):
         kv_arrival(o).wait_recv()
@@ -348,55 +400,58 @@
 
     lax.fori_loop(1, 16, kv_end, 0)
     kv_own.wait()
-    whole = xg.at[head]
-    for i in (0, 1, 2, 5, 6, 7):
-        remote(whole, whole, xs_sem.at[i], xy_sem.at[1], seq, up).wait_send()
-    half = xg.at[head, pl.ds(0, ROWS // 2)]
-    for i in (3, 4):
-        remote(half, half, xs_sem.at[i], xy_sem.at[1], seq, up).wait_send()
+    for i in range(4):
+        y_copy(head, i, own_sem.at[0, i], 1, up).wait_send()
+        y_copy(head, i, own_sem.at[1, i], 2, down).wait_send()
+        y_copy(head, i, fwd_sem.at[i], 3, up).wait_send()
+        for kind in range(4):
+            twin_copy(head, i, kind).wait_send()
     for i in (0, 1, 2, 5, 6, 7):
         remote(wmine, wmine, ws_sem.at[i], wy_sem.at[1], seq, up).wait_send()
     half = wo.at[head, pl.ds(0, 64)]
     for i in (3, 4):
         remote(half, half, ws_sem.at[i], wy_sem.at[1], seq, up).wait_send()
-    for i in (0, 1):
-        remote(gmine, gmine, gs_sem.at[i], gr_sem.at[1], znext, head).wait_send()
-    half = gmap.at[sz, pl.ds(0, 128)]
-    for i in (2, 3):
-        remote(half, half, gs_sem.at[i], gr_sem.at[1], znext, head).wait_send()
+    for i in range(2):
+        for kind in range(3):
+            g_copy(0, i, gs_sem.at[kind, i], 1, znext).wait_send()
     remote(srow, sin, hs_sem.at[0], hr_sem.at[0], xnext, head).wait_send()
     remote(ysend, xin, hs_sem.at[1], hr_sem.at[1], xnext, head).wait_send()
     for oy, oc in turns:
         ret_copy(oy, oc).wait_send()
 
 
+def settle_kernel(rowof_ref, mixed_in, kv_in, mixed_out, kv_out, sem, sems):
+    whole = pltpu.make_async_copy(mixed_in, mixed_out, sem)
+    whole.start()
+    moves = [pltpu.make_async_copy(kv_in.at[i], kv_out.at[rowof_ref[i]], sems.at[i]) for i in range(BPS)]
+    for move in moves:
+        move.start()
+    for move in moves:
+        move.wait()
+    whole.wait()
+
+
 def per_device(
     tokens, norm_gain, w_qkv, w_mem_gates, persist_keys, persist_values, alpha_bias, eta_bias,
     w_out, ffn_gain, w_gate, w_up, w_down, segment_ids, block_table,
 ):
-    seq = lax.axis_index("seq")
-    ids = segment_ids.reshape(-1, SPAN)[:, 0]
-    keep_all = jnp.concatenate([jnp.zeros((1,), F32), (ids[1:] == ids[:-1]).astype(F32)])
-    keep = lax.dynamic_slice_in_dim(keep_all, seq * BPS, BPS)
-    slots = jnp.arange(BPS, dtype=jnp.int32)
-    mine = lax.dynamic_slice_in_dim(block_table, seq * BPS, BPS)
-    place = (mine // BPS) * BPS + slots
-    position = jnp.sum((place[None, :] < place[:, None]).astype(jnp.int32), axis=1)
-    order = jnp.sum(jnp.where(position[None, :] == slots[:, None], slots[None, :], 0), axis=1)
-
     vmem = pl.BlockSpec(memory_space=pltpu.VMEM)
     smem = pl.BlockSpec(memory_space=pltpu.SMEM)
     anywhere = pl.BlockSpec(memory_space=pl.ANY)
     dma = pltpu.SemaphoreType.DMA
-    mixed, arrived = pl.pallas_call(
+    mixed, arrived, rowof = pl.pallas_call(
         layer_kernel,
         out_shape=(
             jax.ShapeDtypeStruct((ROWS, D), BF16),
             jax.ShapeDtypeStruct((BPS, SPAN, 2 * HD), BF16),
+            jax.ShapeDtypeStruct((BPS,), jnp.int32),
         ),
-        in_specs=[smem] * 4 + [vmem] * 8 + [anywhere] * 3,
-        out_specs=(vmem, anywhere),
+        in_specs=[smem] * 3 + [anywhere] + [vmem] * 9 + [anywhere] * 3,
+        out_specs=(vmem, anywhere, smem),
         scratch_shapes=[
+            pltpu.SMEM((BPS * SPAN,), jnp.int32),
+            pltpu.SMEM((1024,), jnp.int32),
+            pltpu.SMEM((BPS,), jnp.int32),
             pltpu.VMEM((8, ROWS, D), BF16),
             pltpu.VMEM((8, HD, D), BF16),
             pltpu.VMEM((D, FF), BF16),
@@ -415,13 +470,13 @@
             pltpu.VMEM((2 * HD, HD), BF16),
             pltpu.VMEM((8, ROWS, HD), BF16),
             pltpu.VMEM((8, ROWS, HD), BF16),
-            pltpu.VMEM((8, HD), F32),
             pltpu.VMEM((ROWS, D), F32),
             pltpu.VMEM((ROWS, D), BF16),
-            dma((3,)), dma,
+            pltpu.VMEM((ROWS, FF), BF16),
+            dma((5,)), dma,
+            dma((2, 4)), dma((4,)), dma((4, 4)), dma((4, 4)), dma((4, 4)),
             dma((8,)), dma((4,)), dma((4,)),
-            dma((8,)), dma((4,)), dma((4,)),
-            dma((4,)), dma((4,)),
+            dma((3, 2)), dma((4, 2)),
             dma((2,)), dma((2,)),
             dma((8,)), dma((8,)),
             dma((16,)), dma((16,)),
@@ -430,17 +485,22 @@
             collective_id=0, has_side_effects=True, vmem_limit_bytes=56 * MIB
         ),
     )(
-        keep, order, alpha_bias, eta_bias,
-        tokens, norm_gain.reshape(1, D), w_qkv.reshape(D, 3 * HD), w_mem_gates.reshape(3, HD),
+        alpha_bias, eta_bias, block_table, segment_ids,
+        block_table.reshape(4, 128), tokens, norm_gain.reshape(1, D), w_qkv.reshape(D, 3 * HD), w_mem_gates.reshape(3, HD),
         persist_keys, persist_values, w_out, ffn_gain.reshape(1, D),
         w_gate, w_up, w_down,
     )
 
-    wanted = seq * BPS + slots
-    blocks = jnp.arange(block_table.shape[0], dtype=jnp.int32)
-    block_of = jnp.sum(jnp.where(block_table[None, :] == wanted[:, None], blocks[None, :], 0), axis=1)
-    spot = jnp.sum((block_of[None, :] < block_of[:, None]).astype(jnp.int32), axis=1)
-    return mixed, arrived[spot]
+    return pl.pallas_call(
+        settle_kernel,
+        out_shape=(
+            jax.ShapeDtypeStruct((ROWS, D), BF16),
+            jax.ShapeDtypeStruct((BPS, SPAN, 2 * HD), BF16),
+        ),
+        in_specs=[smem, anywhere, anywhere],
+        out_specs=(anywhere, anywhere),
+        scratch_shapes=[dma, dma((BPS,))],
+    )(rowof, mixed, arrived)
 
 
 def solution(mesh):

time: 84.5 us -> 119 us (1.41)
  Pallas kernels: 73.1 us -> 117 us
  local copies, waits for them, and re-layouts: 6.27 us -> 0 us
  other arithmetic: 2.87 us -> 0 us
    pallas_call x0 -> x1, Pallas kernels: none -> 49.7 us  [per_device(): pl.pallas_call(settle_kernel, out_shape=(jax.ShapeDtypeStruct((ROWS, D),...]
    pallas_call x1, Pallas kernels: 73.1 us -> 67.5 us  [per_device(): pl.pallas_call(layer_kernel, out_shape=(jax.ShapeDtypeStruct((ROWS, D), B...]
    gather x1 -> x0, local copies, waits for them, and re-layouts: 2.81 us -> none  [per_device(): return (mixed, arrived[spot])]
    unnamed x1 -> x0, local copies, waits for them, and re-layouts: 1.87 us -> none
    reduce_sum x4 -> x0, other arithmetic: 1.86 us -> none  [the longest x1 0.87 us: per_device(): jnp.sum(jnp.where(block_table[None, :] == wanted[:, None], blocks[None, :...]
where the time goes in v1:
time: 119 us
  Pallas kernels  117 us (98%)
  between operations  2.09 us (2%)
    pallas_call x1, Pallas kernels, per_device(): pl.pallas_call(layer_kernel, out_shape=(jax.ShapeDtypeStruct((ROWS, D), B...  67.5 us
    pallas_call x1, Pallas kernels, per_device(): pl.pallas_call(settle_kernel, out_shape=(jax.ShapeDtypeStruct((ROWS, D),...  49.7 us

profile of v1, /device:TPU:1, one launch (start us, length us, event | category | flops | bytes accessed | tf_op | source)
XLA Modules:
  0.0 119.3 jit_solution(9748562539294906903)
XLA Ops:
  1.9 67.5 %shard_map.158 = (bf16[256,1024]{1,0:T(8,128)(2,1)}, bf16[32,64,256]{2,1,0:T(8,128)(2,1)}, s32[32]{0:T(128)}) custom-call(f32[1]{0:T(128)S(6)} %copy.17.ab_ref, f32[1]{0:T(128)S(6)} %copy.18.eb_ref, s32[512]{0:T(512)} %table_ref.1, s32[32768]{0:T(1024)} %ids_hbm.1, s32[4,128]{1,0:T(4,128)} %bitcast.6, bf16[256,1024]{1,0:T(8,128)(2,1)} %tokens_ref.1, ...), custom_call_target="tpu_custom_call" | custom-call | tf_op jit(solution)/shard_map/pallas_call | solution.py:442
  69.4 49.7 %shard_map.159 = (bf16[256,1024]{1,0:T(8,128)(2,1)}, bf16[32,64,256]{2,1,0:T(8,128)(2,1)}) custom-call(s32[32]{0:T(128)} %get-tuple-element.5.rowof_ref, bf16[256,1024]{1,0:T(8,128)(2,1)} %get-tuple-element.6.mixed_in, bf16[32,64,256]{2,1,0:T(8,128)(2,1)} %get-tuple-element.7.kv_in), custom_call_target="tpu_custom_call" | custom-call | tf_op jit(solution)/shard_map/pallas_call | solution.py:494

commit v2 on v1

--- a/solution.py
+++ b/solution.py
@@ -420,15 +420,24 @@
         ret_copy(oy, oc).wait_send()
 
 
-def settle_kernel(rowof_ref, mixed_in, kv_in, mixed_out, kv_out, sem, sems):
-    whole = pltpu.make_async_copy(mixed_in, mixed_out, sem)
-    whole.start()
-    moves = [pltpu.make_async_copy(kv_in.at[i], kv_out.at[rowof_ref[i]], sems.at[i]) for i in range(BPS)]
-    for move in moves:
-        move.start()
-    for move in moves:
-        move.wait()
-    whole.wait()
+def settle_kernel(rowof_ref, mixed_in, kv_in, mixed_out, kv_out, mixed_at, kv_at, in_sem, out_sem, kv_sem):
+    halves = [pl.ds(i * 128, 128) for i in range(2)]
+    groups = [pl.ds(i * 4, 4) for i in range(8)]
+    loads = [pltpu.make_async_copy(kv_in.at[g], kv_at.at[g], in_sem.at[i]) for i, g in enumerate(groups)]
+    loads += [pltpu.make_async_copy(mixed_in.at[h], mixed_at.at[h], in_sem.at[8 + i]) for i, h in enumerate(halves)]
+    for load in loads:
+        load.start()
+    stores = [pltpu.make_async_copy(kv_at.at[i], kv_out.at[rowof_ref[i]], kv_sem.at[i]) for i in range(BPS)]
+    whole = [pltpu.make_async_copy(mixed_at.at[h], mixed_out.at[h], out_sem.at[i]) for i, h in enumerate(halves)]
+    for i in range(8):
+        loads[i].wait()
+        for b in range(4):
+            stores[4 * i + b].start()
+    for i in range(2):
+        loads[8 + i].wait()
+        whole[i].start()
+    for store in stores + whole:
+        store.wait()
 
 
 def per_device(
@@ -499,7 +508,11 @@
         ),
         in_specs=[smem, anywhere, anywhere],
         out_specs=(anywhere, anywhere),
-        scratch_shapes=[dma, dma((BPS,))],
+        scratch_shapes=[
+            pltpu.VMEM((ROWS, D), BF16),
+            pltpu.VMEM((BPS, SPAN, 2 * HD), BF16),
+            dma((10,)), dma((2,)), dma((BPS,)),
+        ],
     )(rowof, mixed, arrived)
 
 

time: 119 us -> 73 us (0.61)
  Pallas kernels: 117 us -> 70.7 us
    pallas_call x1, Pallas kernels: 49.7 us -> 3.21 us  [per_device(): pl.pallas_call(settle_kernel, out_shape=(jax.ShapeDtypeStruct((ROWS, D),...]
where the time goes in v2:
time: 73 us; the launch traced here: 72.8 us
  Pallas kernels  70.7 us (97%)
  between operations  2.09 us (3%)
    pallas_call x1, Pallas kernels, per_device(): pl.pallas_call(layer_kernel, out_shape=(jax.ShapeDtypeStruct((ROWS, D), B...  67.5 us
    pallas_call x1, Pallas kernels, per_device(): pl.pallas_call(settle_kernel, out_shape=(jax.ShapeDtypeStruct((ROWS, D),...  3.21 us

profile of v2, /device:TPU:1, one launch (start us, length us, event | category | flops | bytes accessed | tf_op | source)
XLA Modules:
  0.0 72.8 jit_solution(3758673217024011896)
XLA Ops:
  1.9 67.5 %shard_map.158 = (bf16[256,1024]{1,0:T(8,128)(2,1)}, bf16[32,64,256]{2,1,0:T(8,128)(2,1)}, s32[32]{0:T(128)}) custom-call(f32[1]{0:T(128)S(6)} %copy.17.ab_ref, f32[1]{0:T(128)S(6)} %copy.18.eb_ref, s32[512]{0:T(512)} %table_ref.1, s32[32768]{0:T(1024)} %ids_hbm.1, s32[4,128]{1,0:T(4,128)} %bitcast.6, bf16[256,1024]{1,0:T(8,128)(2,1)} %tokens_ref.1, ...), custom_call_target="tpu_custom_call" | custom-call | tf_op jit(solution)/shard_map/pallas_call | solution.py:451
  69.4 3.2 %shard_map.159 = (bf16[256,1024]{1,0:T(8,128)(2,1)}, bf16[32,64,256]{2,1,0:T(8,128)(2,1)}) custom-call(s32[32]{0:T(128)} %get-tuple-element.5.rowof_ref, bf16[256,1024]{1,0:T(8,128)(2,1)} %get-tuple-element.6.mixed_in, bf16[32,64,256]{2,1,0:T(8,128)(2,1)} %get-tuple-element.7.kv_in), custom_call_target="tpu_custom_call" | custom-call | tf_op jit(solution)/shard_map/pallas_call | solution.py:503

commit v3 on v2

--- a/solution.py
+++ b/solution.py
@@ -41,10 +41,10 @@
 
 def layer_kernel(
     ab_ref, eb_ref, table_ref, ids_hbm,
-    wide_table_ref, tokens_ref, ngain_ref, wq_ref, wmg_ref, pk_ref, pv_ref, wout_ref, fgain_ref,
-    wg_hbm, wu_hbm, wd_hbm,
+    wide_table_ref, tokens_ref, ngain_ref, wmg_ref, pk_ref, pv_ref, fgain_ref,
+    wq_hbm, wout_hbm, wg_hbm, wu_hbm, wd_hbm,
     mixed_ref, kv_hbm, rowof_ref,
-    ids, before, order, xg, wo, wg, wu, wd, kvbuf, kvsend, rm, rs, pt, gmap, pz, srow, sin, ysend, xin,
+    ids, before, order, wq_ref, xg, wo, wg, wu, wd, kvbuf, kvsend, rm, rs, pt, gmap, pz, srow, sin, ysend, xin,
     retsend, ret, resid, ffn_in, hid,
     local_sem, kvl_sem, own_sem, fwd_sem, tws_sem, yr_sem, twr_sem, ws_sem, wy_sem, wc_sem,
     gs_sem, gr_sem, hs_sem, hr_sem, as_sem, ar_sem, ks_sem, kr_sem,
@@ -76,7 +76,9 @@
         pltpu.make_async_copy(ids_hbm.at[pl.ds(mine_ids, BPS * SPAN)], ids, local_sem.at[3]),
         pltpu.make_async_copy(ids_hbm.at[pl.ds(prior_ids, 1024)], before, local_sem.at[4]),
     ]
-    for load in id_loads:
+    wq_load = pltpu.make_async_copy(wq_hbm, wq_ref, local_sem.at[5])
+    wout_load = pltpu.make_async_copy(wout_hbm, wo.at[head], local_sem.at[6])
+    for load in id_loads + [wq_load, wout_load]:
         load.start()
 
     barrier = pltpu.get_barrier_semaphore()
@@ -158,57 +160,69 @@
         there = jnp.where(block + seq == 0, -1, there)
         return jnp.where(here == there, 1.0, 0.0)
 
-    def process(chips):
-        work = []
-        for yp in chips:
-            x = xg[pl.ds(2 * yp, 2)].reshape(2 * ROWS, D)
-            proj = jnp.dot(x, wq_ref[...], preferred_element_type=F32)
-            q = unit(proj[:, :HD]) * HD ** (-0.5)
-            k = unit(proj[:, HD : 2 * HD]) * HD ** (-0.5)
-            v = proj[:, 2 * HD :]
-            wmg = wmg_ref[...].astype(F32)
-            theta = sigmoid(jnp.sum(v * wmg[0:1], axis=-1, keepdims=True)) * (1.0 / SPAN)
-            mean_v = jnp.mean(v.reshape(8, SPAN, HD), axis=1)
-            alpha = sigmoid(jnp.sum(mean_v * wmg[1:2], axis=-1, keepdims=True) + ab_ref[0])
-            eta = sigmoid(jnp.sum(mean_v * wmg[2:3], axis=-1, keepdims=True) + eb_ref[0])
-            qb, kb = q.astype(BF16), k.astype(BF16)
-            kvbuf[pl.ds(yp * 8, 8), :, :HD] = kb.reshape(8, SPAN, HD)
-            kvbuf[pl.ds(yp * 8, 8), :, HD:] = v.astype(BF16).reshape(8, SPAN, HD)
-            for half in range(2):
-                work.append([yp, half * 4, qb, k, kb, v, theta, alpha, eta, eye_m, eye_s, []])
-        for step in range(4):
-            for item in work:
-                yp, first_block, qb, k, kb, v, theta, alpha, eta, memory, moment, reads = item
-                b = first_block + step
+    def join(later, earlier):
+        return jnp.concatenate(compose(later, earlier), axis=1)
+
+    def project(x, first_block, yp):
+        proj = jnp.dot(x, wq_ref[...], preferred_element_type=F32)
+        q = unit(proj[:, :HD]) * HD ** (-0.5)
+        k = unit(proj[:, HD : 2 * HD]) * HD ** (-0.5)
+        v = proj[:, 2 * HD :]
+        blocks = x.shape[0] // SPAN
+        wmg = wmg_ref[...].astype(F32)
+        theta = sigmoid(jnp.sum(v * wmg[0:1], axis=-1, keepdims=True)) * (1.0 / SPAN)
+        mean_v = jnp.mean(v.reshape(blocks, SPAN, HD), axis=1)
+        alpha = sigmoid(jnp.sum(mean_v * wmg[1:2], axis=-1, keepdims=True) + ab_ref[0])
+        eta = sigmoid(jnp.sum(mean_v * wmg[2:3], axis=-1, keepdims=True) + eb_ref[0])
+        qb, kb = q.astype(BF16), k.astype(BF16)
+        kvbuf[pl.ds(yp * 8 + first_block, blocks), :, :HD] = kb.reshape(blocks, SPAN, HD)
+        kvbuf[pl.ds(yp * 8 + first_block, blocks), :, HD:] = v.astype(BF16).reshape(blocks, SPAN, HD)
+        return qb, k, kb, v, theta, alpha, eta
+
+    def chains(work, steps):
+        states = [[eye_m, eye_s, []] for _ in work]
+        for step in range(steps):
+            for (yp, block, at, (qb, k, kb, v, theta, alpha, eta)), state in zip(work, states):
+                b = at + step
                 rows = slice(b * SPAN, (b + 1) * SPAN)
-                keep = keep_of(yp, b)
+                memory, moment, reads = state
+                keep = keep_of(yp, block + step)
                 held = keep * memory + (1.0 - keep) * fresh
                 both = mm(jnp.concatenate([qb[rows], kb[rows]], axis=0), held)
                 reads.append(both[:SPAN])
                 wide_v = jnp.concatenate([zero_rows, v[rows]], axis=1)
                 push = theta[rows] * (wide_v - both[SPAN:])
                 moment = eta[b : b + 1] * (keep * moment) + mm(k[rows].T, push)
-                memory = (1.0 - alpha[b : b + 1]) * held + moment
-                item[9], item[10] = memory, moment
-        for i in range(0, len(work), 2):
-            yp = work[i][0]
-            even = jnp.concatenate([work[i][9], work[i][10]], axis=0)
-            odd = jnp.concatenate([work[i + 1][9], work[i + 1][10]], axis=0)
-            tmap, tshift = compose(odd, even)
-            pt[yp, :, :256] = tmap
-            pt[yp, :, 256:] = tshift
-            read_even = jnp.concatenate(work[i][11], axis=0)
-            read_odd = jnp.concatenate(work[i + 1][11], axis=0)
-            omap, oshift = compose(read_odd, even)
-            rm[2 * yp] = read_even[:, :256].astype(BF16)
-            rs[2 * yp] = read_even[:, 256:]
-            rm[2 * yp + 1] = omap.astype(BF16)
-            rs[2 * yp + 1] = oshift
+                state[0] = (1.0 - alpha[b : b + 1]) * held + moment
+                state[1] = moment
+        return [
+            (jnp.concatenate(state[:2], axis=0), jnp.concatenate(state[2], axis=0)) for state in states
+        ]
+
+    def append(first, second):
+        return join(second[0], first[0]), jnp.concatenate([first[1], join(second[1], first[0])], axis=0)
+
+    def settle(yp, even, odd):
+        tmap, reads = append(even, odd)
+        pt[yp] = tmap
+        rm[pl.ds(2 * yp, 2)] = reads[:, :256].astype(BF16).reshape(2, ROWS, 2 * HD)
+        rs[pl.ds(2 * yp, 2)] = reads[:, 256:].reshape(2, ROWS, HD)
+
+    def process(chips):
+        work = []
+        for yp in chips:
+            made = project(xg[pl.ds(2 * yp, 2)].reshape(2 * ROWS, D), 0, yp)
+            work += [(yp, 0, 0, made), (yp, 4, 4, made)]
+        done = chains(work, 4)
+        for i, yp in enumerate(chips):
+            settle(yp, done[2 * i], done[2 * i + 1])
 
     def twin_in(kind):
         for i in range(4):
             twin_copy(others[kind], i, kind).wait_recv()
 
+    wq_load.wait()
+    wout_load.wait()
     twin_in(0)
     process([y])
     for i in range(4):
@@ -226,11 +240,19 @@
     for i in (0, 3, 1, 2):
         y_copy(slots[3], i, own_sem.at[0, 0], 3, up).wait_recv()
         twin_copy(slots[3], i, 3).start()
+    far = (y + 2) % 4
+    here = project(xg[2 * far + c], 4 * c, far)
     twin_in(3)
-    process([(y + 2) % 4])
-
-    def join(later, earlier):
-        return jnp.concatenate(compose(later, earlier), axis=1)
+    there = project(xg[2 * far + 1 - c], 4 * (1 - c), far)
+    done = chains(
+        [(far, 4 * c, 0, here), (far, 4 * c + 2, 2, here), (far, 4 - 4 * c, 0, there), (far, 6 - 4 * c, 2, there)], 2
+    )
+    here, there = append(done[0], done[1]), append(done[2], done[3])
+    settle(
+        far,
+        [jnp.where(c == 0, a, b) for a, b in zip(here, there)],
+        [jnp.where(c == 0, b, a) for a, b in zip(here, there)],
+    )
 
     first = join(pt[1], pt[0])
     total = join(join(pt[3], pt[2]), first)
@@ -243,7 +265,6 @@
         g_copy(0, i, gs_sem.at[0, i], 1, znext).start()
         g_copy(0, 1 - i, gs_sem.at[1, 1 - i], 2, zprev).start()
 
-    wo[head] = wout_ref[...]
     wmine = wo.at[head]
     remote(wmine, wmine, ws_sem.at[1], wy_sem.at[1], seq, up).start()
     remote(wmine, wmine, ws_sem.at[2], wy_sem.at[2], seq, down).start()
@@ -264,6 +285,23 @@
         return 0
 
     lax.fori_loop(0, BPS, place, 0)
+
+    def kv_copy(o):
+        to = ((sx + o // 4) % 4) * 4 + (sz + o % 4) % 4
+        return remote(
+            kvsend.at[pl.ds(2 * to, 2)], kv_hbm.at[pl.ds(2 * seq, 2)], ks_sem.at[o], kr_sem.at[o], to, head
+        )
+
+    def kv_arrival(o):
+        source = ((sx + 4 - o // 4) % 4) * 4 + (sz + 4 - o % 4) % 4
+        return remote(
+            kvsend.at[pl.ds(2 * source, 2)], kv_hbm.at[pl.ds(2 * source, 2)], ks_sem.at[o], kr_sem.at[o], source, head
+        )
+
+    kv_own = pltpu.make_async_copy(kvsend.at[pl.ds(2 * seq, 2)], kv_hbm.at[pl.ds(2 * seq, 2)], kvl_sem)
+    kv_own.start()
+    for o in (4, 8, 12):
+        kv_copy(o).start()
 
     g_copy(3, 0, gs_sem.at[0, 0], 1, znext).wait_recv()
     g_copy(3, 0, gs_sem.at[2, 0], 3, znext).start()
@@ -282,6 +320,9 @@
     total = join(bjoin(gmap[3], gmap[2]), low)
     srow[...] = total[:, 256:].astype(BF16)
     remote(srow, sin, hs_sem.at[0], hr_sem.at[0], xnext, head).start()
+
+    for o in (1, 2, 3):
+        kv_copy(o).start()
 
     @pl.when(sz == 1)
     def _():
@@ -317,26 +358,6 @@
 
         lax.fori_loop(0, 4, fold_all, 0)
 
-    def kv_copy(o):
-        to = (seq + o) % 16
-        return remote(
-            kvsend.at[pl.ds(2 * to, 2)], kv_hbm.at[pl.ds(2 * seq, 2)], ks_sem.at[o], kr_sem.at[o], to, head
-        )
-
-    def kv_arrival(o):
-        source = (seq + 16 - o) % 16
-        return remote(
-            kvsend.at[pl.ds(2 * source, 2)], kv_hbm.at[pl.ds(2 * source, 2)], ks_sem.at[o], kr_sem.at[o], source, head
-        )
-
-    def kv_start(o, _):
-        kv_copy(o).start()
-        return 0
-
-    lax.fori_loop(1, 16, kv_start, 0)
-    kv_own = pltpu.make_async_copy(kvsend.at[pl.ds(2 * seq, 2)], kv_hbm.at[pl.ds(2 * seq, 2)], kvl_sem)
-    kv_own.start()
-
     wfar = wo.at[((y + 2) % 4) * 2 + c]
     remote(wfar, wfar, ws_sem.at[1], wy_sem.at[3], seq, up).wait_recv()
     remote(wfar, wfar, ws_sem.at[7], wc_sem.at[3], seq, twin).start()
@@ -362,32 +383,32 @@
     for oy, oc in turns:
         retsend[oy * 2 + oc] = answer(((y + oy) % 4) * 2 + (c + oc) % 2)
         ret_copy(oy, oc).start()
+    for o in (10, 5, 6, 7, 9, 11, 13, 14, 15):
+        kv_copy(o).start()
     ret[head] = answer(head)
 
+    total = tokens_ref[...].astype(F32)
     for p, off in ((0, 0), (1, 3), (2, 1), (3, 2)):
-        other = wo.at[((y + off) % 4) * 2 + 1 - c]
+        yp = (y + off) % 4
+        other = wo.at[2 * yp + 1 - c]
         remote(other, other, ws_sem.at[0], wc_sem.at[p], seq, twin).wait_recv()
+        if p > 0:
+            ret_arrival((4 - off) % 4, 0).wait_recv()
+        ret_arrival((4 - off) % 4, 1).wait_recv()
+        left = jnp.concatenate([ret[2 * yp], ret[2 * yp + 1]], axis=1)
+        total = total + jnp.dot(left, wo[pl.ds(2 * yp, 2)].reshape(2 * HD, D), preferred_element_type=F32)
     for load in loads:
         load.wait()
-    for oy, oc in turns:
-        ret_arrival(oy, oc).wait_recv()
-
-    total = tokens_ref[...].astype(F32)
-    for i in range(4):
-        left = jnp.concatenate([ret[2 * i], ret[2 * i + 1]], axis=1)
-        total = total + jnp.dot(left, wo[2 * i : 2 * i + 2].reshape(2 * HD, D), preferred_element_type=F32)
+
     resid[...] = total
     scale = lax.rsqrt(jnp.mean(total * total, axis=-1, keepdims=True) + EPS)
     ffn_in[...] = (total * scale * fgain_ref[...]).astype(BF16)
 
-    def widen(t, _):
-        cols = pl.ds(pl.multiple_of(t * 256, 256), 256)
+    for t in range(FF // 256):
+        cols = slice(t * 256, (t + 1) * 256)
         gate = jnp.dot(ffn_in[...], wg[:, cols], preferred_element_type=F32)
         upper = jnp.dot(ffn_in[...], wu[:, cols], preferred_element_type=F32)
         hid[:, cols] = (gate / (1.0 + jnp.exp(-gate)) * upper).astype(BF16)
-        return 0
-
-    lax.fori_loop(0, FF // 256, widen, 0)
     for t in range(4):
         cols = slice(t * 256, (t + 1) * 256)
         down_part = jnp.dot(hid[...], wd[:, cols], preferred_element_type=F32)
@@ -455,12 +476,13 @@
             jax.ShapeDtypeStruct((BPS, SPAN, 2 * HD), BF16),
             jax.ShapeDtypeStruct((BPS,), jnp.int32),
         ),
-        in_specs=[smem] * 3 + [anywhere] + [vmem] * 9 + [anywhere] * 3,
+        in_specs=[smem] * 3 + [anywhere] + [vmem] * 7 + [anywhere] * 5,
         out_specs=(vmem, anywhere, smem),
         scratch_shapes=[
             pltpu.SMEM((BPS * SPAN,), jnp.int32),
             pltpu.SMEM((1024,), jnp.int32),
             pltpu.SMEM((BPS,), jnp.int32),
+            pltpu.VMEM((D, 3 * HD), BF16),
             pltpu.VMEM((8, ROWS, D), BF16),
             pltpu.VMEM((8, HD, D), BF16),
             pltpu.VMEM((D, FF), BF16),
@@ -482,7 +504,7 @@
             pltpu.VMEM((ROWS, D), F32),
             pltpu.VMEM((ROWS, D), BF16),
             pltpu.VMEM((ROWS, FF), BF16),
-            dma((5,)), dma,
+            dma((7,)), dma,
             dma((2, 4)), dma((4,)), dma((4, 4)), dma((4, 4)), dma((4, 4)),
             dma((8,)), dma((4,)), dma((4,)),
             dma((3, 2)), dma((4, 2)),
@@ -495,9 +517,9 @@
         ),
     )(
         alpha_bias, eta_bias, block_table, segment_ids,
-        block_table.reshape(4, 128), tokens, norm_gain.reshape(1, D), w_qkv.reshape(D, 3 * HD), w_mem_gates.reshape(3, HD),
-        persist_keys, persist_values, w_out, ffn_gain.reshape(1, D),
-        w_gate, w_up, w_down,
+        block_table.reshape(4, 128), tokens, norm_gain.reshape(1, D), w_mem_gates.reshape(3, HD),
+        persist_keys, persist_values, ffn_gain.reshape(1, D),
+        w_qkv.reshape(D, 3 * HD), w_out, w_gate, w_up, w_down,
     )
 
     return pl.pallas_call(

time: 73 us -> 69.5 us (0.952)
  Pallas kernels: 70.7 us -> 66.7 us
    pallas_call x1, Pallas kernels: 67.5 us -> 63.5 us  [per_device(): pl.pallas_call(layer_kernel, out_shape=(jax.ShapeDtypeStruct((ROWS, D), B...]
where the time goes in v3:
time: 69.5 us; the launch traced here: 68.8 us
  Pallas kernels  66.7 us (96%)
  between operations  2.09 us (3%)
    pallas_call x1, Pallas kernels, per_device(): pl.pallas_call(layer_kernel, out_shape=(jax.ShapeDtypeStruct((ROWS, D), B...  63.5 us
    pallas_call x1, Pallas kernels, per_device(): pl.pallas_call(settle_kernel, out_shape=(jax.ShapeDtypeStruct((ROWS, D),...  3.21 us

profile of v3, /device:TPU:1, one launch (start us, length us, event | category | flops | bytes accessed | tf_op | source)
XLA Modules:
  0.0 68.8 jit_solution(13985201265896571658)
XLA Ops:
  1.9 63.5 %shard_map.158 = (bf16[256,1024]{1,0:T(8,128)(2,1)}, bf16[32,64,256]{2,1,0:T(8,128)(2,1)}, s32[32]{0:T(128)}) custom-call(f32[1]{0:T(128)S(6)} %copy.17.ab_ref, f32[1]{0:T(128)S(6)} %copy.18.eb_ref, s32[512]{0:T(512)} %table_ref.1, s32[32768]{0:T(1024)} %ids_hbm.1, s32[4,128]{1,0:T(4,128)} %bitcast.6, bf16[256,1024]{1,0:T(8,128)(2,1)} %tokens_ref.1, ...), custom_call_target="tpu_custom_call" | custom-call | tf_op jit(solution)/shard_map/pallas_call | solution.py:472
  65.4 3.2 %shard_map.159 = (bf16[256,1024]{1,0:T(8,128)(2,1)}, bf16[32,64,256]{2,1,0:T(8,128)(2,1)}) custom-call(s32[32]{0:T(128)} %get-tuple-element.5.rowof_ref, bf16[256,1024]{1,0:T(8,128)(2,1)} %get-tuple-element.6.mixed_in, bf16[32,64,256]{2,1,0:T(8,128)(2,1)} %get-tuple-element.7.kv_in), custom_call_target="tpu_custom_call" | custom-call | tf_op jit(solution)/shard_map/pallas_call | solution.py:525

commit v4 on v3

--- a/solution.py
+++ b/solution.py
@@ -12,6 +12,7 @@
 SPAN = 64
 ROWS = 256
 PIECE = 64
+HALF = 128
 TOKENS = 32768
 BPS = 32
 EPS = 1e-05
@@ -321,7 +322,7 @@
     srow[...] = total[:, 256:].astype(BF16)
     remote(srow, sin, hs_sem.at[0], hr_sem.at[0], xnext, head).start()
 
-    for o in (1, 2, 3):
+    for o in (1, 2, 3, 13, 14, 15):
         kv_copy(o).start()
 
     @pl.when(sz == 1)
@@ -358,6 +359,9 @@
 
         lax.fori_loop(0, 4, fold_all, 0)
 
+    for o in (10, 9, 11):
+        kv_copy(o).start()
+
     wfar = wo.at[((y + 2) % 4) * 2 + c]
     remote(wfar, wfar, ws_sem.at[1], wy_sem.at[3], seq, up).wait_recv()
     remote(wfar, wfar, ws_sem.at[7], wc_sem.at[3], seq, twin).start()
@@ -365,54 +369,58 @@
     remote(ysend, xin, hs_sem.at[1], hr_sem.at[1], xnext, head).wait_recv()
     enter = xin[...]
 
-    def answer(j):
-        recalled = jnp.dot(rm[j], enter, preferred_element_type=F32) + rs[j]
+    def answer(j, rows):
+        recalled = jnp.dot(rm[j, rows], enter, preferred_element_type=F32) + rs[j, rows]
         return unit(recalled).astype(BF16)
 
-    def ret_copy(oy, oc):
-        o = oy * 2 + oc
+    def ret_copy(t, oy, oc):
+        o, rows = oy * 2 + oc, pl.ds(t * HALF, HALF)
         to = ((y + oy) % 4) * 2 + (c + oc) % 2
-        return remote(retsend.at[o], ret.at[head], as_sem.at[o], ar_sem.at[o], seq, to)
-
-    def ret_arrival(oy, oc):
-        o = oy * 2 + oc
+        return remote(retsend.at[o, rows], ret.at[head, rows], as_sem.at[t, o], ar_sem.at[t, o], seq, to)
+
+    def ret_arrival(t, oy, oc):
+        o, rows = oy * 2 + oc, pl.ds(t * HALF, HALF)
         source = ((y + 4 - oy) % 4) * 2 + (c + oc) % 2
-        return remote(retsend.at[o], ret.at[source], as_sem.at[o], ar_sem.at[o], seq, source)
+        return remote(retsend.at[o, rows], ret.at[source, rows], as_sem.at[t, o], ar_sem.at[t, o], seq, source)
 
     turns = [(2, 0), (2, 1), (1, 0), (1, 1), (3, 0), (3, 1), (0, 1)]
-    for oy, oc in turns:
-        retsend[oy * 2 + oc] = answer(((y + oy) % 4) * 2 + (c + oc) % 2)
-        ret_copy(oy, oc).start()
-    for o in (10, 5, 6, 7, 9, 11, 13, 14, 15):
-        kv_copy(o).start()
-    ret[head] = answer(head)
-
-    total = tokens_ref[...].astype(F32)
+    for t in range(2):
+        rows = pl.ds(t * HALF, HALF)
+        for oy, oc in turns:
+            retsend[oy * 2 + oc, rows] = answer(((y + oy) % 4) * 2 + (c + oc) % 2, rows)
+            ret_copy(t, oy, oc).start()
+        ret[head, rows] = answer(head, rows)
+        if t == 0:
+            for o in (5, 6, 7):
+                kv_copy(o).start()
+
     for p, off in ((0, 0), (1, 3), (2, 1), (3, 2)):
-        yp = (y + off) % 4
-        other = wo.at[2 * yp + 1 - c]
+        other = wo.at[((y + off) % 4) * 2 + 1 - c]
         remote(other, other, ws_sem.at[0], wc_sem.at[p], seq, twin).wait_recv()
-        if p > 0:
-            ret_arrival((4 - off) % 4, 0).wait_recv()
-        ret_arrival((4 - off) % 4, 1).wait_recv()
-        left = jnp.concatenate([ret[2 * yp], ret[2 * yp + 1]], axis=1)
-        total = total + jnp.dot(left, wo[pl.ds(2 * yp, 2)].reshape(2 * HD, D), preferred_element_type=F32)
     for load in loads:
         load.wait()
-
-    resid[...] = total
-    scale = lax.rsqrt(jnp.mean(total * total, axis=-1, keepdims=True) + EPS)
-    ffn_in[...] = (total * scale * fgain_ref[...]).astype(BF16)
-
-    for t in range(FF // 256):
-        cols = slice(t * 256, (t + 1) * 256)
-        gate = jnp.dot(ffn_in[...], wg[:, cols], preferred_element_type=F32)
-        upper = jnp.dot(ffn_in[...], wu[:, cols], preferred_element_type=F32)
-        hid[:, cols] = (gate / (1.0 + jnp.exp(-gate)) * upper).astype(BF16)
-    for t in range(4):
-        cols = slice(t * 256, (t + 1) * 256)
-        down_part = jnp.dot(hid[...], wd[:, cols], preferred_element_type=F32)
-        mixed_ref[:, cols] = (resid[:, cols] + down_part).astype(BF16)
+    for t in range(2):
+        rows = slice(t * HALF, (t + 1) * HALF)
+        total = tokens_ref[rows].astype(F32)
+        for off in (0, 3, 1, 2):
+            yp = (y + off) % 4
+            if off > 0:
+                ret_arrival(t, (4 - off) % 4, 0).wait_recv()
+            ret_arrival(t, (4 - off) % 4, 1).wait_recv()
+            left = jnp.concatenate([ret[2 * yp, rows], ret[2 * yp + 1, rows]], axis=1)
+            total = total + jnp.dot(left, wo[pl.ds(2 * yp, 2)].reshape(2 * HD, D), preferred_element_type=F32)
+        resid[rows] = total
+        scale = lax.rsqrt(jnp.mean(total * total, axis=-1, keepdims=True) + EPS)
+        ffn_in[rows] = (total * scale * fgain_ref[...]).astype(BF16)
+        for i in range(FF // 256):
+            cols = slice(i * 256, (i + 1) * 256)
+            gate = jnp.dot(ffn_in[rows], wg[:, cols], preferred_element_type=F32)
+            upper = jnp.dot(ffn_in[rows], wu[:, cols], preferred_element_type=F32)
+            hid[rows, cols] = (gate / (1.0 + jnp.exp(-gate)) * upper).astype(BF16)
+        for i in range(4):
+            cols = slice(i * 256, (i + 1) * 256)
+            down_part = jnp.dot(hid[rows], wd[:, cols], preferred_element_type=F32)
+            mixed_ref[rows, cols] = (resid[rows, cols] + down_part).astype(BF16)
 
     def kv_end(o, _):
         kv_arrival(o).wait_recv()
@@ -437,28 +445,18 @@
             g_copy(0, i, gs_sem.at[kind, i], 1, znext).wait_send()
     remote(srow, sin, hs_sem.at[0], hr_sem.at[0], xnext, head).wait_send()
     remote(ysend, xin, hs_sem.at[1], hr_sem.at[1], xnext, head).wait_send()
-    for oy, oc in turns:
-        ret_copy(oy, oc).wait_send()
-
-
-def settle_kernel(rowof_ref, mixed_in, kv_in, mixed_out, kv_out, mixed_at, kv_at, in_sem, out_sem, kv_sem):
-    halves = [pl.ds(i * 128, 128) for i in range(2)]
-    groups = [pl.ds(i * 4, 4) for i in range(8)]
-    loads = [pltpu.make_async_copy(kv_in.at[g], kv_at.at[g], in_sem.at[i]) for i, g in enumerate(groups)]
-    loads += [pltpu.make_async_copy(mixed_in.at[h], mixed_at.at[h], in_sem.at[8 + i]) for i, h in enumerate(halves)]
-    for load in loads:
-        load.start()
-    stores = [pltpu.make_async_copy(kv_at.at[i], kv_out.at[rowof_ref[i]], kv_sem.at[i]) for i in range(BPS)]
-    whole = [pltpu.make_async_copy(mixed_at.at[h], mixed_out.at[h], out_sem.at[i]) for i, h in enumerate(halves)]
-    for i in range(8):
-        loads[i].wait()
-        for b in range(4):
-            stores[4 * i + b].start()
-    for i in range(2):
-        loads[8 + i].wait()
-        whole[i].start()
-    for store in stores + whole:
-        store.wait()
+    for t in range(2):
+        for oy, oc in turns:
+            ret_copy(t, oy, oc).wait_send()
+
+
+def settle_kernel(rowof_ref, mixed_in, kv_in, mixed_out, kv_out, sem, kv_sem):
+    moves = [pltpu.make_async_copy(kv_in.at[i], kv_out.at[rowof_ref[i]], kv_sem.at[i]) for i in range(BPS)]
+    moves.append(pltpu.make_async_copy(mixed_in, mixed_out, sem))
+    for move in moves:
+        move.start()
+    for move in moves:
+        move.wait()
 
 
 def per_device(
@@ -468,6 +466,7 @@
     vmem = pl.BlockSpec(memory_space=pltpu.VMEM)
     smem = pl.BlockSpec(memory_space=pltpu.SMEM)
     anywhere = pl.BlockSpec(memory_space=pl.ANY)
+    hbm = pl.BlockSpec(memory_space=pltpu.HBM)
     dma = pltpu.SemaphoreType.DMA
     mixed, arrived, rowof = pl.pallas_call(
         layer_kernel,
@@ -476,7 +475,7 @@
             jax.ShapeDtypeStruct((BPS, SPAN, 2 * HD), BF16),
             jax.ShapeDtypeStruct((BPS,), jnp.int32),
         ),
-        in_specs=[smem] * 3 + [anywhere] + [vmem] * 7 + [anywhere] * 5,
+        in_specs=[smem] * 3 + [hbm] + [vmem] * 7 + [hbm] * 5,
         out_specs=(vmem, anywhere, smem),
         scratch_shapes=[
             pltpu.SMEM((BPS * SPAN,), jnp.int32),
@@ -509,7 +508,7 @@
             dma((8,)), dma((4,)), dma((4,)),
             dma((3, 2)), dma((4, 2)),
             dma((2,)), dma((2,)),
-            dma((8,)), dma((8,)),
+            dma((2, 8)), dma((2, 8)),
             dma((16,)), dma((16,)),
         ],
         compiler_params=pltpu.CompilerParams(
@@ -528,13 +527,9 @@
             jax.ShapeDtypeStruct((ROWS, D), BF16),
             jax.ShapeDtypeStruct((BPS, SPAN, 2 * HD), BF16),
         ),
-        in_specs=[smem, anywhere, anywhere],
-        out_specs=(anywhere, anywhere),
-        scratch_shapes=[
-            pltpu.VMEM((ROWS, D), BF16),
-            pltpu.VMEM((BPS, SPAN, 2 * HD), BF16),
-            dma((10,)), dma((2,)), dma((BPS,)),
-        ],
+        in_specs=[smem, vmem, vmem],
+        out_specs=(hbm, hbm),
+        scratch_shapes=[dma, dma((BPS,))],
     )(rowof, mixed, arrived)
 
 

time: 69.5 us -> 68.9 us (level)
  no operation moved by 1% of the time
where the time goes in v4:
time: 68.9 us; the launch traced here: 68.6 us
  Pallas kernels  66.5 us (97%)
  between operations  2.09 us (3%)
    pallas_call x1, Pallas kernels, per_device(): pl.pallas_call(layer_kernel, out_shape=(jax.ShapeDtypeStruct((ROWS, D), B...  63.6 us
    pallas_call x1, Pallas kernels, per_device(): pl.pallas_call(settle_kernel, out_shape=(jax.ShapeDtypeStruct((ROWS, D),...  2.83 us

profile of v4, /device:TPU:1, one launch (start us, length us, event | category | flops | bytes accessed | tf_op | source)
XLA Modules:
  0.0 68.6 jit_solution(1444875652416124469)
XLA Ops:
  1.9 63.6 %shard_map.158 = (bf16[256,1024]{1,0:T(8,128)(2,1)}, bf16[32,64,256]{2,1,0:T(8,128)(2,1)}, s32[32]{0:T(128)}) custom-call(f32[1]{0:T(128)S(6)} %copy.17.ab_ref, f32[1]{0:T(128)S(6)} %copy.18.eb_ref, s32[512]{0:T(512)} %table_ref.1, s32[32768]{0:T(1024)} %ids_hbm.1, s32[4,128]{1,0:T(4,128)} %bitcast.6, bf16[256,1024]{1,0:T(8,128)(2,1)} %tokens_ref.1, ...), custom_call_target="tpu_custom_call" | custom-call | tf_op jit(solution)/shard_map/pallas_call | solution.py:471
  65.6 2.8 %shard_map.159 = (bf16[256,1024]{1,0:T(8,128)(2,1)}, bf16[32,64,256]{2,1,0:T(8,128)(2,1)}) custom-call(s32[32]{0:T(128)} %get-tuple-element.5.rowof_ref, bf16[256,1024]{1,0:T(8,128)(2,1)} %get-tuple-element.6.mixed_in, bf16[32,64,256]{2,1,0:T(8,128)(2,1)} %get-tuple-element.7.kv_in), custom_call_target="tpu_custom_call" | custom-call | tf_op jit(solution)/shard_map/pallas_call | solution.py:524

commit v5 on v4

--- a/solution.py
+++ b/solution.py
@@ -322,7 +322,7 @@
     srow[...] = total[:, 256:].astype(BF16)
     remote(srow, sin, hs_sem.at[0], hr_sem.at[0], xnext, head).start()
 
-    for o in (1, 2, 3, 13, 14, 15):
+    for o in (13, 14, 15, 1, 2, 3):
         kv_copy(o).start()
 
     @pl.when(sz == 1)
@@ -359,8 +359,6 @@
 
         lax.fori_loop(0, 4, fold_all, 0)
 
-    for o in (10, 9, 11):
-        kv_copy(o).start()
 
     wfar = wo.at[((y + 2) % 4) * 2 + c]
     remote(wfar, wfar, ws_sem.at[1], wy_sem.at[3], seq, up).wait_recv()
@@ -391,7 +389,7 @@
             ret_copy(t, oy, oc).start()
         ret[head, rows] = answer(head, rows)
         if t == 0:
-            for o in (5, 6, 7):
+            for o in (10, 9, 11, 5, 6, 7):
                 kv_copy(o).start()
 
     for p, off in ((0, 0), (1, 3), (2, 1), (3, 2)):

time: 68.9 us -> 68.7 us (level); the launches traced: 68.6 us -> 67.6 us
  Pallas kernels: 66.5 us -> 65.5 us
    pallas_call x1, Pallas kernels: 63.6 us -> 62.7 us  [per_device(): pl.pallas_call(layer_kernel, out_shape=(jax.ShapeDtypeStruct((ROWS, D), B...]
where the time goes in v5:
time: 68.7 us; the launch traced here: 67.6 us
  Pallas kernels  65.5 us (95%)
  between operations  2.09 us (3%)
    pallas_call x1, Pallas kernels, per_device(): pl.pallas_call(layer_kernel, out_shape=(jax.ShapeDtypeStruct((ROWS, D), B...  62.7 us
    pallas_call x1, Pallas kernels, per_device(): pl.pallas_call(settle_kernel, out_shape=(jax.ShapeDtypeStruct((ROWS, D),...  2.83 us

profile of v5, /device:TPU:1, one launch (start us, length us, event | category | flops | bytes accessed | tf_op | source)
XLA Modules:
  0.0 67.6 jit_solution(10321347714477197611)
XLA Ops:
  1.9 62.7 %shard_map.158 = (bf16[256,1024]{1,0:T(8,128)(2,1)}, bf16[32,64,256]{2,1,0:T(8,128)(2,1)}, s32[32]{0:T(128)}) custom-call(f32[1]{0:T(128)S(6)} %copy.17.ab_ref, f32[1]{0:T(128)S(6)} %copy.18.eb_ref, s32[512]{0:T(512)} %table_ref.1, s32[32768]{0:T(1024)} %ids_hbm.1, s32[4,128]{1,0:T(4,128)} %bitcast.6, bf16[256,1024]{1,0:T(8,128)(2,1)} %tokens_ref.1, ...), custom_call_target="tpu_custom_call" | custom-call | tf_op jit(solution)/shard_map/pallas_call | solution.py:469
  64.6 2.8 %shard_map.159 = (bf16[256,1024]{1,0:T(8,128)(2,1)}, bf16[32,64,256]{2,1,0:T(8,128)(2,1)}) custom-call(s32[32]{0:T(128)} %get-tuple-element.5.rowof_ref, bf16[256,1024]{1,0:T(8,128)(2,1)} %get-tuple-element.6.mixed_in, bf16[32,64,256]{2,1,0:T(8,128)(2,1)} %get-tuple-element.7.kv_in), custom_call_target="tpu_custom_call" | custom-call | tf_op jit(solution)/shard_map/pallas_call | solution.py:522
